TPU v7x, 256 devices: a whole 4x4x8 slice. The times are simulated.
256 devices in a mesh: seq: 32 (over z_hi, x, core), tensor: 8 (over y, z_lo).
Axes of the slice: x: 4, y: 4, z: 8 (z_hi: 4, z_lo: 2; z = z_hi * 2 + z_lo), core: 2. Of those that a mesh axis runs over, the one named last changes fastest.
Arguments:
- tokens: bfloat16 [4096, 2048], P('seq'), may hold values from -6 to 6
- lengths: int32 [8], replicated, may hold values from 1 to 2048, 4096 in all
- page_table: int32 [256], replicated, may hold values from 0 to 255, each once
- attention_gain: float32 [2048], replicated, may hold values from 0.25 to 1.75
- query_weight: bfloat16 [2048, 2048], P(None, 'tensor')
- key_weight: bfloat16 [2048, 2048], P(None, 'tensor')
- value_weight: bfloat16 [2048, 2048], P(None, 'tensor'), may hold values from -0.125 to 0.125
- out_weight: bfloat16 [2048, 2048], P('tensor'), may hold values from -0.125 to 0.125
- expert_gain: float32 [2048], replicated, may hold values from 0.25 to 1.75
- router_weight: bfloat16 [2048, 64], replicated, may hold values from -0.03125 to 0.03125
- expert_ids: int32 [4096, 8], P('seq'), may hold values from 0 to 63, all different within a row; in each aligned block of 128 rows (0 to 127, 128 to 255, ...) at most 24 rows name the same one
- gate_weight: bfloat16 [64, 2048, 1024], P('seq', None, 'tensor'), may hold values from -0.125 to 0.125
- up_weight: bfloat16 [64, 2048, 1024], P('seq', None, 'tensor'), may hold values from -0.125 to 0.125
- down_weight: bfloat16 [64, 1024, 2048], P('seq', 'tensor'), may hold values from -6 to 6
Outputs:
- layer_out: bfloat16 [4096, 2048], P('seq')
- key_cache: bfloat16 [256, 16, 2048], P('seq', None, 'tensor')
- value_cache: bfloat16 [256, 16, 2048], P('seq', None, 'tensor')
Inputs may be any that keep to these rules, and one draw needn't show every extreme that they name: The 8 lengths sum to 4096; the longest is exactly 2048. `page_table`: every page number appears once. `expert_ids`: each token names 8 different experts; among the 128 tokens of one index of seq no expert is named more than 24 times, a bound that some block reaches.
All inputs are finite; a program needn't handle non-finite values.
Results may differ from a plain program's by a relative error of at most 0.023.
Values may be sent and summed in bfloat16 or wider, within the bound.
A program may use at most 128 MiB of HBM per device.

v0:
```python
import jax
import jax.numpy as jnp
from jax import lax
from jax.sharding import PartitionSpec as P

HEAD_DIM = 128
PAGE = 16
epsilon = 1e-05
rope_base = 10000.0


def rms_scale(matrix, scaling):
    mean_square = jnp.mean(matrix * matrix, axis=-1, keepdims=True)
    return matrix * lax.rsqrt(mean_square + epsilon) * scaling


def segment_info(lengths, places):
    starts = jnp.cumsum(lengths) - lengths
    inside = (places[:, None] >= starts[None, :]).astype(jnp.int32)
    segment = jnp.sum(inside, axis=1) - 1
    slot_ids = jnp.arange(starts.shape[0], dtype=jnp.int32)
    seg_start = jnp.sum(
        jnp.where(slot_ids[None, :] == segment[:, None], starts[None, :], 0), axis=1
    )
    return (segment, places - seg_start)


def rotate(matrix, position):
    half_dim = matrix.shape[-1] // 2
    frequency = jnp.exp(
        -jnp.log(rope_base) * jnp.arange(half_dim, dtype=jnp.float32) * (2.0 / matrix.shape[-1])
    )
    angles = position.astype(jnp.float32)[:, None] * frequency[None, :]
    cosine = jnp.cos(angles)[:, None, :]
    sine_part = jnp.sin(angles)[:, None, :]
    first_half = matrix[..., :half_dim]
    second = matrix[..., half_dim:]
    return jnp.concatenate(
        [first_half * cosine - second * sine_part, second * cosine + first_half * sine_part],
        axis=-1,
    )


def local(
    tokens,
    lengths,
    page_table,
    attention_gain,
    query_weight,
    key_weight,
    value_weight,
    out_weight,
    expert_gain,
    router_weight,
    expert_ids,
    gate_weight,
    up_weight,
    down_weight,
):
    row_count = tokens.shape[0]
    feature_count = tokens.shape[1]
    span_size = query_weight.shape[1]
    head_count = span_size // HEAD_DIM
    shard_id = lax.axis_index("seq")
    places = shard_id * row_count + jnp.arange(row_count, dtype=jnp.int32)
    segment, position = segment_info(lengths, places)
    stream = tokens.astype(jnp.float32)
    normed = rms_scale(stream, attention_gain).astype(jnp.bfloat16)
    queries = rotate(
        jnp.dot(normed, query_weight, preferred_element_type=jnp.float32).reshape(
            row_count, head_count, HEAD_DIM
        ),
        position,
    ).astype(jnp.bfloat16)
    key_rows = (
        rotate(
            jnp.dot(normed, key_weight, preferred_element_type=jnp.float32).reshape(
                row_count, head_count, HEAD_DIM
            ),
            position,
        )
        .astype(jnp.bfloat16)
        .reshape(row_count, span_size)
    )
    value_rows = jnp.dot(normed, value_weight, preferred_element_type=jnp.float32).astype(
        jnp.bfloat16
    )
    page_rows = row_count // PAGE
    my_pages = shard_id * page_rows + jnp.arange(page_rows, dtype=jnp.int32)
    owned = (page_table[None, :] == my_pages[:, None]).astype(jnp.bfloat16)
    score_scale = HEAD_DIM ** (-0.5)
    state = (
        jnp.full((head_count, row_count), -1e30, jnp.float32),
        jnp.zeros((head_count, row_count), jnp.float32),
        jnp.zeros((head_count, row_count, HEAD_DIM), jnp.float32),
    )
    key_piece = lax.all_gather(key_rows, "seq", axis=0, tiled=True)
    value_piece = lax.all_gather(value_rows, "seq", axis=0, tiled=True)
    piece_rows = key_piece.shape[0]
    key_pages = jnp.dot(
        owned,
        key_piece.reshape(piece_rows // PAGE, PAGE * span_size),
        preferred_element_type=jnp.float32,
    )
    value_pages = jnp.dot(
        owned,
        value_piece.reshape(piece_rows // PAGE, PAGE * span_size),
        preferred_element_type=jnp.float32,
    )
    row_peak, row_total, weighted = state
    piece_rows = key_piece.shape[0]
    key_places = jnp.arange(piece_rows, dtype=jnp.int32)
    key_segments, _ = segment_info(lengths, key_places)
    scores = (
        jnp.einsum(
            "qhd,khd->hqk",
            queries,
            key_piece.reshape(piece_rows, head_count, HEAD_DIM),
            preferred_element_type=jnp.float32,
        )
        * score_scale
    )
    allowed = (
        (segment[:, None] == key_segments[None, :]) & (key_places[None, :] <= places[:, None])
    )[None]
    new_peak = jnp.maximum(row_peak, jnp.max(jnp.where(allowed, scores, -1e30), axis=-1))
    raised = jnp.where(allowed, jnp.exp(scores - new_peak[:, :, None]), 0.0)
    row_total = jnp.sum(raised, axis=-1)
    weighted = jnp.einsum(
        "hqk,khd->hqd",
        raised.astype(jnp.bfloat16),
        value_piece.reshape(piece_rows, head_count, HEAD_DIM),
        preferred_element_type=jnp.float32,
    )
    state = (new_peak, row_total, weighted)
    state, key_pages, value_pages = (state, key_pages, value_pages)
    _, row_total, weighted = state
    attended = (
        jnp.transpose(weighted / row_total[:, :, None], (1, 0, 2))
        .reshape(row_count, span_size)
        .astype(jnp.bfloat16)
    )
    head_part = jnp.dot(attended, out_weight, preferred_element_type=jnp.float32)
    hidden = stream + lax.psum(head_part.astype(jnp.bfloat16), "tensor").astype(jnp.float32)
    moe_input = rms_scale(hidden, expert_gain).astype(jnp.bfloat16)
    expert_count = router_weight.shape[1]
    probability = jax.nn.softmax(
        jnp.dot(moe_input, router_weight, preferred_element_type=jnp.float32), axis=-1
    )
    expert_range = jnp.arange(expert_count, dtype=jnp.int32)
    chosen = jnp.sum(
        jnp.where(
            expert_ids[:, :, None] == expert_range[None, None, :], probability[:, None, :], 0.0
        ),
        axis=-1,
    )
    top_count = expert_ids.shape[1]
    flat_ids = expert_ids.reshape(-1)
    onehot = (flat_ids[:, None] == expert_range[None, :]).astype(jnp.int32)
    slot_rank = jnp.sum(jnp.cumsum(onehot, axis=0) * onehot, axis=1) - 1
    members = lax.axis_size("tensor")
    sources = lax.axis_size("seq")
    local_count = gate_weight.shape[0]
    base_room = row_count * top_count * 3 // (2 * expert_count)
    capacity = members * ((base_room + members - 1) // members)
    owners = jnp.arange(row_count * top_count, dtype=jnp.int32) // top_count
    slot_index = flat_ids * capacity + slot_rank
    row_table = (
        jnp.full((expert_count * capacity,), row_count, jnp.int32).at[slot_index].set(owners)
    )
    padded = jnp.concatenate([moe_input, jnp.zeros((1, feature_count), jnp.bfloat16)], axis=0)
    outgoing = padded[row_table].reshape(sources, local_count, capacity, feature_count)
    arrived = lax.all_to_all(outgoing, "seq", split_axis=0, concat_axis=0, tiled=True)
    gate_out = jnp.einsum(
        "sjnd,jdf->sjnf", arrived, gate_weight, preferred_element_type=jnp.float32
    )
    up_out = jnp.einsum("sjnd,jdf->sjnf", arrived, up_weight, preferred_element_type=jnp.float32)
    activation = (jax.nn.silu(gate_out) * up_out).astype(jnp.bfloat16)
    returned = lax.all_to_all(
        jnp.einsum(
            "sjnf,jfd->sjnd", activation, down_weight, preferred_element_type=jnp.float32
        ).astype(jnp.bfloat16),
        "seq",
        split_axis=0,
        concat_axis=0,
        tiled=True,
    )
    flat_rows = returned.reshape(expert_count * capacity, feature_count)
    picked = flat_rows[slot_index].astype(jnp.float32)
    mixture_part = jnp.sum(
        picked.reshape(row_count, top_count, feature_count) * chosen[:, :, None], axis=1
    )
    mixture = lax.psum(mixture_part.astype(jnp.bfloat16), "tensor").astype(jnp.float32)
    layer_out = (hidden + mixture).astype(jnp.bfloat16)
    key_cache = key_pages.reshape(page_rows, PAGE, span_size).astype(jnp.bfloat16)
    value_cache = value_pages.reshape(page_rows, PAGE, span_size).astype(jnp.bfloat16)
    return (layer_out, key_cache, value_cache)


def solution(mesh):
    return jax.shard_map(
        local,
        mesh=mesh,
        in_specs=(
            P("seq", None),
            P(),
            P(),
            P(),
            P(None, "tensor"),
            P(None, "tensor"),
            P(None, "tensor"),
            P("tensor", None),
            P(),
            P(),
            P("seq", None),
            P("seq", None, "tensor"),
            P("seq", None, "tensor"),
            P("seq", "tensor", None),
        ),
        out_specs=(P("seq", None), P("seq", None, "tensor"), P("seq", None, "tensor")),
        check_vma=False,
    )
```

profile of v0, /device:TPU:2, one launch (start us, length us, event | category | flops | bytes accessed | tf_op | source)
XLA Modules:
  0.0 651.1 jit_solution(417091453030510193)
XLA Ops:
  7.3 0.9 reduce-window.19
  8.2 0.7 bitcast_subtract_fusion
  9.1 1.2 fusion.34
  10.3 1.8 fusion.75
  12.2 1.8 fusion.77
  14.0 0.3 multiply_cosine_fusion
  14.3 0.3 fusion.79
  14.8 0.7 copy.74
  15.7 2.2 convolution_convert_fusion.3
  18.5 18.0 %reduce-window.20 = s32[64,8,128]{2,1,0:T(8,128)S(1)} reduce-window(s32[64,8,128]{2,1,0:T(8,128)S(1)} %fusion.52, s32[]{:T(128)} %constant.30.clone.1), window={size=1x1x128 pad=0_0x0_0x127_0}, to_apply=%region_9.10 | reduce-window | flops 8323072 | bytes 524292 | tf_op jit(solution)/shard_map/reduce-window.1
  36.6 0.1 copy.80
  37.3 0.5 fusion.11
  37.8 35.6 %all-gather.3.cloned.1.call-done = bf16[4096,256]{0,1:T(8,128)(2,1)} async-done(((bf16[128,256]{0,1:T(8,128)(2,1)}), bf16[4096,256]{0,1:T(8,128)(2,1)}) %all-gather.3.cloned.1.call-update) | async-done | bytes 2097168 | tf_op jit(solution)/shard_map/all_gather | solution.py:97
  73.4 2.9 select_reduce_fusion
  76.3 1.9 copy-done.2
  78.2 1.1 fusion.5
  79.3 49.4 %all-gather.5.cloned.1.call-done = bf16[4096,256]{1,0:T(8,128)(2,1)} async-done(((bf16[128,256]{1,0:T(8,128)(2,1)}), bf16[4096,256]{1,0:T(8,128)(2,1)}) %all-gather.5.cloned.1.call-update) | async-done | bytes 2097168 | tf_op jit(solution)/shard_map/all_gather | solution.py:98
  128.7 4.1 copy.95
  132.8 3.9 fusion.31
  136.7 1.1 convolution_convert_fusion
  137.9 4.3 scatter_custom_fusion
  142.3 74.3 %all-reduce.4.cloned.1.call-done = bf16[128,2048]{1,0:T(8,128)(2,1)} async-done(((bf16[128,2048]{1,0:T(8,128)(2,1)}), bf16[128,2048]{1,0:T(8,128)(2,1)}) %all-reduce.4.cloned.1.call-update) | async-done | bytes 524304 | tf_op jit(solution)/shard_map/psum | solution.py:144
  216.6 1.3 multiply_reduce_fusion
  217.9 1.3 multiply_convert_fusion
  219.2 0.8 copy-done.6
  220.0 7.1 %gather_fusion = bf16[1536,2048]{1,0:T(8,128)(2,1)} fusion(bf16[129,2048]{1,0:T(8,128)(2,1)S(1)} %concatenate.13, s32[2048]{0:T(1024)S(1)} %pad_clamp_fusion), kind=kCustom, calls=%fused_computation | custom fusion | bytes 12589056 | tf_op jit(solution)/shard_map/gather | solution.py:172
  227.1 149.0 %all_to_all.10 = bf16[32,2,24,2048]{3,2,1,0:T(8,128)(2,1)S(1)} all-to-all(bf16[32,2,24,2048]{3,2,1,0:T(8,128)(2,1)} %bitcast.85), channel_id=1, replica_groups=mesh['seq'=32,'tensor'=8] {'seq'}, dimensions={0} | all-to-all | bytes 12582912 | tf_op jit(solution)/shard_map/all_to_all | solution.py:173
  376.1 2.7 copy-done.5
  378.8 1.9 fusion.13
  380.7 8.9 %convert_bitcast_fusion = bf16[32,2,24,2048]{3,2,0,1:T(8,128)(2,1)} fusion(bf16[2,128,2048]{2,1,0:T(8,128)(2,1)S(1)} %copy-done, bf16[32,2,24,2048]{3,2,1,0:T(8,128)(2,1)} %copy-done.5, bf16[2,2048,128]{2,1,0:T(8,128)(2,1)S(1)} %copy-done.14, f32[32,2,24,128]{3,2,0,1:T(8,128)S(1)} %fusion.13), kind=kOutput, calls=%fused_computation.5 | convolution fusion | flops 1614938112 | bytes 15466496 | tf_op jit(solution)/shard_map/sjnf,jfd->sjnd/dot_general | solution.py:180
  389.6 6.6 %copy.84 = bf16[32,2,24,2048]{3,2,1,0:T(8,128)(2,1)} copy(bf16[32,2,24,2048]{3,2,0,1:T(8,128)(2,1)} %convert_bitcast_fusion) | data formatting | bytes 12582912 | tf_op jit(solution)/shard_map/convert_element_type | solution.py:182
  396.2 6.6 %all-to-all-start.1 = ((bf16[32,2,24,2048]{3,2,1,0:T(8,128)(2,1)}), bf16[32,2,24,2048]{3,2,1,0:T(8,128)(2,1)}, u32[]{:S(2)}, u32[]{:S(2)}) async-start(bf16[32,2,24,2048]{3,2,1,0:T(8,128)(2,1)} %copy.84), calls=%async_computation.1 | async-start | bytes 12582912 | tf_op jit(solution)/shard_map/all_to_all | solution.py:179
  402.8 0.3 all-reduce.6.cloned.1.call-start
  403.1 3.3 copy.86
  406.4 2.4 reshape.277
  408.8 4.1 copy.87
  412.8 0.3 fusion.81
  413.4 130.8 %all-to-all-done.1 = bf16[32,2,24,2048]{3,2,1,0:T(8,128)(2,1)} async-done(((bf16[32,2,24,2048]{3,2,1,0:T(8,128)(2,1)}), bf16[32,2,24,2048]{3,2,1,0:T(8,128)(2,1)}, u32[]{:S(2)}, u32[]{:S(2)}) %all-to-all-start.1) | async-done | bytes 6291488 | tf_op jit(solution)/shard_map/all_to_all | solution.py:179
  544.2 12.4 %gather_fusion.1 = bf16[1024,2048]{1,0:T(8,128)(2,1)} fusion(bf16[1536,2048]{1,0:T(8,128)(2,1)} %bitcast.22, s32[1024]{0:T(1024)S(1)} %broadcast_clamp_fusion), kind=kCustom, calls=%fused_computation.1 | custom fusion | bytes 8392704 | tf_op jit(solution)/shard_map/gather | solution.py:189
  556.6 7.5 %fusion = bf16[128,2048]{1,0:T(8,128)(2,1)} fusion(bf16[1024,2048]{1,0:T(8,128)(2,1)} %gather_fusion.1, f32[128,8]{1,0:T(8,128)S(1)} %copy.85), kind=kLoop, calls=%fused_computation.4 | loop fusion | flops 6029312 | bytes 4722688 | tf_op jit(solution)/shard_map/reduce_sum | solution.py:190
  564.1 2.2 convolution_convert_fusion.2
  566.3 0.7 copy.89
  567.0 2.4 reshape.278
  569.4 3.4 copy.88
  572.7 0.6 convolution_convert_fusion.1
  573.4 0.7 copy.90
  574.0 68.2 %all-reduce.6.cloned.1.call-done = bf16[128,2048]{1,0:T(8,128)(2,1)} async-done(((bf16[128,2048]{1,0:T(8,128)(2,1)}), bf16[128,2048]{1,0:T(8,128)(2,1)}) %all-reduce.6.cloned.1.call-update) | async-done | bytes 524304 | tf_op jit(solution)/shard_map/psum | solution.py:193
  642.2 2.4 add_convert_fusion
  (76 shorter events, 2.1 us)
Async XLA Ops:
  7.2 373.5 %copy-start = (bf16[2,128,2048]{2,1,0:T(8,128)(2,1)S(1)}, bf16[2,128,2048]{2,1,0:T(8,128)(2,1)}, u32[]{:S(2)}) copy-start(bf16[2,128,2048]{2,1,0:T(8,128)(2,1)} %param.27) | copy-start | bytes 3145732
  7.2 8.5 %copy-start.4 = (bf16[128,2048]{1,0:T(8,128)(2,1)S(1)}, bf16[128,2048]{1,0:T(8,128)(2,1)}, u32[]{:S(2)}) copy-start(bf16[128,2048]{1,0:T(8,128)(2,1)} %param.14) | copy-start | bytes 1572868
  7.2 8.5 %copy-start.15 = (f32[2048]{0:T(1024)S(1)}, f32[2048]{0:T(1024)}, u32[]{:S(2)}) copy-start(f32[2048]{0:T(1024)} %param.17) | copy-start | bytes 24580
  7.2 66.1 %all-gather.3.cloned.1.call-start = ((), (), s32[]{:S(2)}) async-start(), calls=%async_computation.2 | async-start | bytes 2162688 | tf_op jit(solution)/shard_map/all_gather | solution.py:97
  10.3 7.7 %copy-start.10 = (s32[128,8]{0,1:T(8,128)S(1)}, s32[128,8]{0,1:T(8,128)}, u32[]{:S(2)}) copy-start(s32[128,8]{0,1:T(8,128)} %param.24) | copy-start | bytes 12292
  15.6 113.1 %all-gather.5.cloned.1.call-start = ((), (), s32[]{:S(2)}) async-start(), calls=%async_computation.3 | async-start | bytes 2162688 | tf_op jit(solution)/shard_map/all_gather | solution.py:98
  17.9 198.7 %all-reduce.4.cloned.1.call-start = ((), (), s32[]{:S(2)}) async-start(), calls=%async_computation.4 | async-start | bytes 1048576 | tf_op jit(solution)/shard_map/psum | solution.py:144
  76.3 1.9 copy-start.2
  132.8 4.0 copy-start.8
  132.8 85.1 %copy-start.11 = (f32[2048]{0:T(1024)S(1)}, f32[2048]{0:T(1024)}, u32[]{:S(2)}) copy-start(f32[2048]{0:T(1024)} %param.22) | copy-start | bytes 24580
  219.2 0.8 copy-start.6
  227.1 151.7 %copy-start.13 = (bf16[2,2048,128]{2,1,0:T(8,128)(2,1)S(1)}, bf16[2,2048,128]{2,1,0:T(8,128)(2,1)}, u32[]{:S(2)}) copy-start(bf16[2,2048,128]{2,1,0:T(8,128)(2,1)} %param.25) | copy-start | bytes 3145732
  376.1 2.7 copy-start.5
  378.8 1.9 copy-start.14
  396.2 148.0 %all-to-all-start.1 = ((bf16[32,2,24,2048]{3,2,1,0:T(8,128)(2,1)}), bf16[32,2,24,2048]{3,2,1,0:T(8,128)(2,1)}, u32[]{:S(2)}, u32[]{:S(2)}) async-start(bf16[32,2,24,2048]{3,2,1,0:T(8,128)(2,1)} %copy.84), calls=%async_computation.1 | async-start | bytes 12582912 | tf_op jit(solution)/shard_map/all_to_all | solution.py:179
  402.8 239.4 %all-reduce.6.cloned.1.call-start = ((), (), s32[]{:S(2)}) async-start(), calls=%async_computation.5 | async-start | bytes 1048576 | tf_op jit(solution)/shard_map/psum | solution.py:193
  406.3 6.5 copy-start.7
  406.4 6.5 copy-start.9
  556.6 7.5 %copy-start.12 = (s32[256]{0:T(256)S(1)}, s32[256]{0:T(256)}, u32[]{:S(2)}) copy-start(s32[256]{0:T(256)} %param.16) | copy-start | bytes 3076
  556.6 10.4 %copy-start.3 = (bf16[4096,256]{1,0:T(8,128)(2,1)S(1)}, bf16[4096,256]{1,0:T(8,128)(2,1)}, u32[]{:S(2)}) copy-start(bf16[4096,256]{1,0:T(8,128)(2,1)} %all-gather.5.cloned.1.call-done) | copy-start | bytes 6291460
  569.3 75.2 %copy-start.1 = (bf16[2,128,2048]{2,1,0:T(8,128)(2,1)S(1)}, bf16[2,128,2048]{2,1,0:T(8,128)(2,1)}, u32[]{:S(2)}) copy-start(bf16[2,128,2048]{2,1,0:T(8,128)(2,1)} %param.27) | copy-start | bytes 3145732
Sparse Core Ops, SparseCore 0:
  15.7 57.5 all-gather.2
  76.5 52.1 all-gather.4
  138.0 78.5 all-reduce.3
  564.2 77.9 all-reduce.5
where the time goes:
time: 652 us; the launch traced here: 651 us
  waiting for transfers between devices  358 us (55%)
  blocking collectives  149 us (23%)
  local copies, waits for them, and re-layouts  58.9 us (9%)
  other arithmetic  36 us (6%)
  matrix products  27.7 us (4%)
  between operations  14.2 us (2%)
  starting transfers between devices  6.95 us (1%)
    all_to_all x1, blocking collectives, local(): lax.all_to_all(outgoing, 'seq', split_axis=0, concat_axis=0, tiled=True)  149 us
    all_to_all x1, waiting for transfers between devices, local(): lax.all_to_all(jnp.einsum('sjnf,jfd->sjnd', activation, down_weight, pref...  131 us
    psum x1, waiting for transfers between devices, local(): lax.psum(head_part.astype(jnp.bfloat16), 'tensor').astype(jnp.float32)  74.3 us
    psum x1, waiting for transfers between devices, local(): lax.psum(mixture_part.astype(jnp.bfloat16), 'tensor').astype(jnp.float32)  68.2 us
    all_gather x1, waiting for transfers between devices, local(): value_piece = lax.all_gather(value_rows, 'seq', axis=0, tiled=True)  49.4 us
    all_gather x1, waiting for transfers between devices, local(): key_piece = lax.all_gather(key_rows, 'seq', axis=0, tiled=True)  35.6 us
    another operation x5, other arithmetic  19.2 us
  transfers between devices with their start and end apart: 5, of which 5 were waited for; matrix products, arithmetic and copies ran while one was open for 8% of the time, Pallas kernels for 0%

commit v1 on v0

--- a/solution.py
+++ b/solution.py
@@ -7,6 +7,13 @@
 PAGE = 16
 epsilon = 1e-05
 rope_base = 10000.0
+
+
+def swapped_in(array, mesh_axis, dim):
+    size = lax.axis_size(mesh_axis)
+    blocks = jnp.stack([array for _ in range(size)])
+    blocks = lax.all_to_all(blocks, mesh_axis, split_axis=0, concat_axis=0)
+    return jnp.concatenate(blocks, axis=dim)
 
 
 def rms_scale(matrix, scaling):
@@ -95,7 +102,7 @@
         jnp.zeros((head_count, row_count, HEAD_DIM), jnp.float32),
     )
     key_piece = lax.all_gather(key_rows, "seq", axis=0, tiled=True)
-    value_piece = lax.all_gather(value_rows, "seq", axis=0, tiled=True)
+    value_piece = swapped_in(value_rows, "seq", 0)
     piece_rows = key_piece.shape[0]
     key_pages = jnp.dot(
         owned,

time: 652 us -> 624 us (0.957)
  waiting for transfers between devices: 358 us -> 298 us
  other arithmetic: 36 us -> 53.5 us
  starting transfers between devices: 6.95 us -> 18.7 us
    all_gather x1 -> x0, waiting for transfers between devices: 49.4 us -> none  [local(): value_piece = lax.all_gather(value_rows, 'seq', axis=0, tiled=True)]
    another operation x5, other arithmetic: 19.2 us -> 33.8 us
    all_gather x1, waiting for transfers between devices: 35.6 us -> 21 us  [local(): key_piece = lax.all_gather(key_rows, 'seq', axis=0, tiled=True)]
    all_to_all x0 -> x1, starting transfers between devices: none -> 11.6 us  [swapped_in(): blocks = lax.all_to_all(blocks, mesh_axis, split_axis=0, concat_axis=0)]
    another operation x2 -> x5, local copies, waits for them, and re-layouts: 0.09 us -> 8.15 us  [the longest x1 2.37 us: local(): value_piece.reshape(piece_rows // PAGE, PAGE * span_size)]
  transfers between devices with their start and end apart: 5 -> 5, of which waited for: 5 -> 4; matrix products, arithmetic and copies ran while one was open for 8% -> 11% of each run, Pallas kernels for 0% -> 0%
where the time goes in v1:
time: 624 us; the launch traced here: 622 us
  waiting for transfers between devices  298 us (48%)
  blocking collectives  149 us (24%)
  local copies, waits for them, and re-layouts  62.9 us (10%)
  other arithmetic  53.5 us (9%)
  matrix products  24.9 us (4%)
  starting transfers between devices  18.7 us (3%)
  between operations  14.3 us (2%)
    all_to_all x1, blocking collectives, local(): lax.all_to_all(outgoing, 'seq', split_axis=0, concat_axis=0, tiled=True)  149 us
    all_to_all x1, waiting for transfers between devices, local(): lax.all_to_all(jnp.einsum('sjnf,jfd->sjnd', activation, down_weight, pref...  135 us
    psum x1, waiting for transfers between devices, local(): lax.psum(head_part.astype(jnp.bfloat16), 'tensor').astype(jnp.float32)  75.8 us
    psum x1, waiting for transfers between devices, local(): lax.psum(mixture_part.astype(jnp.bfloat16), 'tensor').astype(jnp.float32)  66.6 us
    another operation x5, other arithmetic  33.8 us
    all_gather x1, waiting for transfers between devices, local(): key_piece = lax.all_gather(key_rows, 'seq', axis=0, tiled=True)  21 us
  transfers between devices with their start and end apart: 5, of which 4 were waited for; matrix products, arithmetic and copies ran while one was open for 11% of the time, Pallas kernels for 0%

profile of v1, /device:TPU:2, one launch (start us, length us, event | category | flops | bytes accessed | tf_op | source)
XLA Modules:
  0.0 621.5 jit_solution(5432631042168817216)
XLA Ops:
  7.3 1.0 reduce-window.19
  9.5 1.2 fusion.41
  10.7 1.8 fusion.82
  12.6 1.8 fusion.84
  15.3 0.7 copy.73
  16.4 1.6 stack.2
  18.0 11.6 %all-to-all-start = ((bf16[32,128,256]{2,1,0:T(8,128)(2,1)}), bf16[32,128,256]{2,1,0:T(8,128)(2,1)S(1)}, u32[]{:S(2)}, u32[]{:S(2)}) async-start(bf16[32,128,256]{2,1,0:T(8,128)(2,1)} %stack.2), calls=%async_computation | async-start | bytes 4194304 | tf_op jit(solution)/shard_map/all_to_all | solution.py:15
  30.1 0.7 mul.205
  30.8 0.7 fusion.59
  31.5 31.1 %reduce-window.20 = s32[64,8,128]{2,1,0:T(8,128)S(1)} reduce-window(s32[64,8,128]{2,1,0:T(8,128)} %fusion.59, s32[]{:T(128)} %constant.30.clone.1), window={size=1x1x128 pad=0_0x0_0x127_0}, to_apply=%region_9.10 | reduce-window | flops 8323072 | bytes 524292 | tf_op jit(solution)/shard_map/reduce-window.1
  62.6 0.8 slice.32
  63.4 1.7 copy.79
  65.1 0.7 reduce-window.21
  66.4 1.4 copy.80
  67.8 0.7 convert_reduce_fusion
  68.5 0.9 broadcast_add_fusion
  69.5 2.0 fusion.12
  71.5 21.0 %all-gather.2.cloned.1.call-done = bf16[4096,256]{0,1:T(8,128)(2,1)} async-done(((bf16[128,256]{0,1:T(8,128)(2,1)}), bf16[4096,256]{0,1:T(8,128)(2,1)}) %all-gather.2.cloned.1.call-update) | async-done | bytes 2097168 | tf_op jit(solution)/shard_map/all_gather | solution.py:104
  92.5 3.0 select_reduce_fusion
  95.6 1.9 copy-done.4
  97.5 1.1 fusion.5
  98.6 2.2 reshape.303
  100.8 4.4 fusion.36
  105.3 1.1 convolution_convert_fusion
  106.5 4.3 scatter_custom_fusion
  110.9 75.8 %all-reduce.4.cloned.1.call-done = bf16[128,2048]{1,0:T(8,128)(2,1)} async-done(((bf16[128,2048]{1,0:T(8,128)(2,1)}), bf16[128,2048]{1,0:T(8,128)(2,1)}) %all-reduce.4.cloned.1.call-update) | async-done | bytes 524304 | tf_op jit(solution)/shard_map/psum | solution.py:151
  186.7 1.5 multiply_reduce_fusion
  188.2 1.4 multiply_convert_fusion
  189.6 0.8 copy-done.8
  190.4 7.1 %gather_fusion = bf16[1536,2048]{1,0:T(8,128)(2,1)} fusion(bf16[129,2048]{1,0:T(8,128)(2,1)S(1)} %concatenate.13, s32[2048]{0:T(1024)S(1)} %pad_clamp_fusion), kind=kCustom, calls=%fused_computation | custom fusion | bytes 12589056 | tf_op jit(solution)/shard_map/gather | solution.py:179
  197.5 149.0 %all_to_all.15 = bf16[32,2,24,2048]{3,2,1,0:T(8,128)(2,1)S(1)} all-to-all(bf16[32,2,24,2048]{3,2,1,0:T(8,128)(2,1)} %bitcast.83), channel_id=1, replica_groups=mesh['seq'=32,'tensor'=8] {'seq'}, dimensions={0} | all-to-all | bytes 12582912 | tf_op jit(solution)/shard_map/all_to_all | solution.py:180
  346.5 2.7 copy-done.7
  349.2 1.9 fusion.14
  351.1 8.9 %convert_bitcast_fusion = bf16[32,2,24,2048]{3,2,0,1:T(8,128)(2,1)} fusion(bf16[2,128,2048]{2,1,0:T(8,128)(2,1)S(1)} %copy-done, bf16[32,2,24,2048]{3,2,1,0:T(8,128)(2,1)} %copy-done.7, bf16[2,2048,128]{2,1,0:T(8,128)(2,1)S(1)} %copy-done.21, f32[32,2,24,128]{3,2,0,1:T(8,128)S(1)} %fusion.14), kind=kOutput, calls=%fused_computation.5 | convolution fusion | flops 1614938112 | bytes 15466496 | tf_op jit(solution)/shard_map/sjnf,jfd->sjnd/dot_general | solution.py:187
  360.0 6.6 %copy.83 = bf16[32,2,24,2048]{3,2,1,0:T(8,128)(2,1)} copy(bf16[32,2,24,2048]{3,2,0,1:T(8,128)(2,1)} %convert_bitcast_fusion) | data formatting | bytes 12582912 | tf_op jit(solution)/shard_map/convert_element_type | solution.py:189
  366.6 6.7 %all-to-all-start.2 = ((bf16[32,2,24,2048]{3,2,1,0:T(8,128)(2,1)}), bf16[32,2,24,2048]{3,2,1,0:T(8,128)(2,1)}, u32[]{:S(2)}, u32[]{:S(2)}) async-start(bf16[32,2,24,2048]{3,2,1,0:T(8,128)(2,1)} %copy.83), calls=%async_computation.2 | async-start | bytes 12582912 | tf_op jit(solution)/shard_map/all_to_all | solution.py:186
  373.6 2.4 reshape_reshape.7
  376.0 3.3 copy.87
  379.8 134.8 %all-to-all-done.2 = bf16[32,2,24,2048]{3,2,1,0:T(8,128)(2,1)} async-done(((bf16[32,2,24,2048]{3,2,1,0:T(8,128)(2,1)}), bf16[32,2,24,2048]{3,2,1,0:T(8,128)(2,1)}, u32[]{:S(2)}, u32[]{:S(2)}) %all-to-all-start.2) | async-done | bytes 6291488 | tf_op jit(solution)/shard_map/all_to_all | solution.py:186
  514.6 12.4 %gather_fusion.1 = bf16[1024,2048]{1,0:T(8,128)(2,1)} fusion(bf16[1536,2048]{1,0:T(8,128)(2,1)} %bitcast.21, s32[1024]{0:T(1024)S(1)} %broadcast_clamp_fusion), kind=kCustom, calls=%fused_computation.1 | custom fusion | bytes 8392704 | tf_op jit(solution)/shard_map/gather | solution.py:196
  527.0 7.3 %fusion = bf16[128,2048]{1,0:T(8,128)(2,1)} fusion(bf16[1024,2048]{1,0:T(8,128)(2,1)} %gather_fusion.1, f32[128,8]{1,0:T(8,128)S(1)} %copy.84), kind=kLoop, calls=%fused_computation.4 | loop fusion | flops 6029312 | bytes 4722688 | tf_op jit(solution)/shard_map/reduce_sum | solution.py:197
  535.0 0.7 copy.89
  535.7 3.3 copy.85
  539.0 2.4 reshape.272
  541.3 3.4 copy.86
  545.4 0.7 copy.88
  546.0 66.6 %all-reduce.6.cloned.1.call-done = bf16[128,2048]{1,0:T(8,128)(2,1)} async-done(((bf16[128,2048]{1,0:T(8,128)(2,1)}), bf16[128,2048]{1,0:T(8,128)(2,1)}) %all-reduce.6.cloned.1.call-update) | async-done | bytes 524304 | tf_op jit(solution)/shard_map/psum | solution.py:200
  612.6 2.4 add_convert_fusion
  (90 shorter events, 6.0 us)
Async XLA Ops:
  7.2 343.9 %copy-start = (bf16[2,128,2048]{2,1,0:T(8,128)(2,1)S(1)}, bf16[2,128,2048]{2,1,0:T(8,128)(2,1)}, u32[]{:S(2)}) copy-start(bf16[2,128,2048]{2,1,0:T(8,128)(2,1)} %param.27) | copy-start | bytes 3145732
  7.2 8.9 %copy-start.5 = (bf16[128,2048]{1,0:T(8,128)(2,1)S(1)}, bf16[128,2048]{1,0:T(8,128)(2,1)}, u32[]{:S(2)}) copy-start(bf16[128,2048]{1,0:T(8,128)(2,1)} %param.14) | copy-start | bytes 1572868
  7.2 8.8 %copy-start.22 = (f32[2048]{0:T(1024)S(1)}, f32[2048]{0:T(1024)}, u32[]{:S(2)}) copy-start(f32[2048]{0:T(1024)} %param.17) | copy-start | bytes 24580
  7.2 8.8 %copy-start.19 = (bf16[2048,256]{1,0:T(8,128)(2,1)S(1)}, bf16[2048,256]{1,0:T(8,128)(2,1)}, u32[]{:S(2)}) copy-start(bf16[2048,256]{1,0:T(8,128)(2,1)} %param.20) | copy-start | bytes 3145732
  7.2 85.3 %all-gather.2.cloned.1.call-start = ((), (), s32[]{:S(2)}) async-start(), calls=%async_computation.3 | async-start | bytes 2162688 | tf_op jit(solution)/shard_map/all_gather | solution.py:104
  7.3 3.4 copy-start.17
  8.9 0.5 copy-start.16
  9.0 1.7 copy-start.18
  15.2 14.4 %copy-start.12 = (s32[128,8]{0,1:T(8,128)S(1)}, s32[128,8]{0,1:T(8,128)}, u32[]{:S(2)}) copy-start(s32[128,8]{0,1:T(8,128)} %param.24) | copy-start | bytes 12292
  18.0 80.6 %all-to-all-start = ((bf16[32,128,256]{2,1,0:T(8,128)(2,1)}), bf16[32,128,256]{2,1,0:T(8,128)(2,1)S(1)}, u32[]{:S(2)}, u32[]{:S(2)}) async-start(bf16[32,128,256]{2,1,0:T(8,128)(2,1)} %stack.2), calls=%async_computation | async-start | bytes 4194304 | tf_op jit(solution)/shard_map/all_to_all | solution.py:15
  29.6 157.1 %all-reduce.4.cloned.1.call-start = ((), (), s32[]{:S(2)}) async-start(), calls=%async_computation.4 | async-start | bytes 1048576 | tf_op jit(solution)/shard_map/psum | solution.py:151
  92.5 5.0 copy-start.6
  95.6 1.9 copy-start.4
  98.6 6.7 %copy-start.2 = (bf16[32,128,256]{2,1,0:T(8,128)(2,1)}, bf16[32,128,256]{2,1,0:T(8,128)(2,1)S(1)}, u32[]{:S(2)}) copy-start(bf16[32,128,256]{2,1,0:T(8,128)(2,1)S(1)} %all-to-all-done) | copy-start | bytes 6291460
  100.8 4.5 copy-start.10
  100.8 5.6 copy-start.13
  100.8 87.3 %copy-start.14 = (f32[2048]{0:T(1024)S(1)}, f32[2048]{0:T(1024)}, u32[]{:S(2)}) copy-start(f32[2048]{0:T(1024)} %param.22) | copy-start | bytes 24580
  189.6 0.8 copy-start.8
  197.5 151.7 %copy-start.20 = (bf16[2,2048,128]{2,1,0:T(8,128)(2,1)S(1)}, bf16[2,2048,128]{2,1,0:T(8,128)(2,1)}, u32[]{:S(2)}) copy-start(bf16[2,2048,128]{2,1,0:T(8,128)(2,1)} %param.25) | copy-start | bytes 3145732
  346.5 2.7 copy-start.7
  349.2 1.9 copy-start.21
  366.6 7.0 %copy-start.3 = (bf16[32,128,256]{2,1,0:T(8,128)(2,1)S(1)}, bf16[32,128,256]{2,1,0:T(8,128)(2,1)}, u32[]{:S(2)}) copy-start(bf16[32,128,256]{2,1,0:T(8,128)(2,1)} %copy-done.2) | copy-start | bytes 6291460
  366.6 148.0 %all-to-all-start.2 = ((bf16[32,2,24,2048]{3,2,1,0:T(8,128)(2,1)}), bf16[32,2,24,2048]{3,2,1,0:T(8,128)(2,1)}, u32[]{:S(2)}, u32[]{:S(2)}) async-start(bf16[32,2,24,2048]{3,2,1,0:T(8,128)(2,1)} %copy.83), calls=%async_computation.2 | async-start | bytes 12582912 | tf_op jit(solution)/shard_map/all_to_all | solution.py:186
  373.3 239.3 %all-reduce.6.cloned.1.call-start = ((), (), s32[]{:S(2)}) async-start(), calls=%async_computation.5 | async-start | bytes 1048576 | tf_op jit(solution)/shard_map/psum | solution.py:200
  373.6 5.7 copy-start.9
  373.6 5.7 copy-start.11
  527.0 7.4 %copy-start.15 = (s32[256]{0:T(256)S(1)}, s32[256]{0:T(256)}, u32[]{:S(2)}) copy-start(s32[256]{0:T(256)} %param.16) | copy-start | bytes 3076
  541.3 73.7 %copy-start.1 = (bf16[2,128,2048]{2,1,0:T(8,128)(2,1)S(1)}, bf16[2,128,2048]{2,1,0:T(8,128)(2,1)}, u32[]{:S(2)}) copy-start(bf16[2,128,2048]{2,1,0:T(8,128)(2,1)} %param.27) | copy-start | bytes 3145732
Sparse Core Ops, SparseCore 0:
  16.1 76.3 all-gather.1
  106.6 80.0 all-reduce.3
  534.5 78.0 all-reduce.5
